TPU v7x, 32 devices: a whole 2x2x4 slice. The times are simulated.
32 devices in a mesh: section: 4 (over z), tensor: 8 (over y, x, core).
Axes of the slice: x: 2, y: 2, z: 4, core: 2. Of those that a mesh axis runs over, the one named last changes fastest.
Arguments:
- resid: bfloat16 [32, 3584], P('tensor'), may hold values from -6 to 6
- w_enc: bfloat16 [7168, 3584], P(('section', 'tensor')), may hold values from -0.09375 to 0.09375
- b_enc: float32 [7168], P(('section', 'tensor')), may hold values from -1 to 0.5
- w_dec: bfloat16 [7168, 3584], P(('section', 'tensor')), may hold values from -0.0625 to 0.0625
- b_dec: float32 [3584], replicated, may hold values from -3 to 3
Outputs:
- recon: float32 [32, 3584], P('tensor')
- grad_w_dec: bfloat16 [7168, 3584], P(('section', 'tensor'))
- code_grad: float32 [32, 7168], P(None, ('section', 'tensor'))
- grad_b_dec: float32 [3584], replicated
- loss_value: float32 [], replicated
All inputs are finite; a program needn't handle non-finite values.
Results may differ from a plain program's by a relative error of at most 0.0032.
The roundings to bfloat16 on the way count: a program that leaves them out, or rounds other values in their place, can miss the bound.
Values may be sent and summed in bfloat16 or wider, within the bound.
No kernel may reach another device: no remote copies, remote signals or barrier semaphores. Data moves between devices by JAX's collectives and lax.ppermute only.
A program may use at most 64 MiB of HBM per device.

v0:
```python
import jax
import jax.numpy as jnp
from jax import lax
from jax.sharding import PartitionSpec as P

epsilon = 1e-06


def per_device(resid, w_enc, b_enc, w_dec, b_dec):
    stream = lax.all_gather(resid, "tensor", axis=0, tiled=True)
    preact = (
        lax.dot_general(stream, w_enc, (((1,), (1,)), ((), ())), preferred_element_type=jnp.float32)
        + b_enc
    )
    codes = jnp.maximum(preact, 0.0).astype(jnp.bfloat16)
    codes_f32 = codes.astype(jnp.float32)
    dec_f32 = w_dec.astype(jnp.float32)
    dec_norm = jnp.sqrt(jnp.sum(dec_f32 * dec_f32, axis=1) + epsilon)
    penalty = lax.psum(jnp.sum(codes_f32 * dec_norm), ("section", "tensor"))
    total_rows = stream.shape[0]
    model_width = stream.shape[1]
    shares = lax.psum_scatter(
        jnp.dot(codes, w_dec, preferred_element_type=jnp.float32),
        "tensor",
        scatter_dimension=0,
        tiled=True,
    )
    shares = lax.psum(shares, "section")
    recon = shares + b_dec
    errors = recon - resid.astype(jnp.float32)
    squares, grad_b_dec = lax.psum((jnp.sum(errors * errors), jnp.sum(errors, axis=0)), "tensor")
    err_half = lax.all_gather(errors.astype(jnp.bfloat16), "tensor", axis=0, tiled=True)
    loss_value = (0.5 * squares + penalty) / (total_rows * model_width)
    code_sums = jnp.sum(codes_f32, axis=0)
    grad_w_dec = lax.dot_general(
        codes, err_half, (((0,), (0,)), ((), ())), preferred_element_type=jnp.float32
    )
    grad_w_dec = grad_w_dec + code_sums[:, None] * dec_f32 / dec_norm[:, None]
    code_grad = (
        lax.dot_general(
            err_half, w_dec, (((1,), (1,)), ((), ())), preferred_element_type=jnp.float32
        )
        + dec_norm
    )
    return (recon, grad_w_dec.astype(jnp.bfloat16), code_grad, grad_b_dec, loss_value)


def solution(mesh):
    in_specs = (
        P("tensor", None),
        P(("section", "tensor"), None),
        P(("section", "tensor")),
        P(("section", "tensor"), None),
        P(),
    )
    out_specs = (
        P("tensor", None),
        P(("section", "tensor"), None),
        P(None, ("section", "tensor")),
        P(),
        P(),
    )
    return jax.shard_map(
        per_device, mesh=mesh, in_specs=in_specs, out_specs=out_specs, check_vma=False
    )
```

profile of v0, /device:TPU:0, one launch (start us, length us, event | category | flops | bytes accessed | tf_op | source)
XLA Modules:
  0.0 148.7 jit_solution(17115211651597049739)
XLA Ops:
  7.2 0.0 copy-start
  7.2 0.0 copy-start.2
  7.2 0.0 copy-start.6
  7.2 0.0 all-reduce.4.cloned.1.call-start
  7.2 1.9 %fusion.2 = f32[224]{0:T(256)S(1)} fusion(bf16[224,3584]{1,0:T(8,128)(2,1)} %param.8), kind=kLoop, calls=%fused_computation.5 | loop fusion | flops 2408224 | bytes 1606528 | tf_op jit(solution)/shard_map/reduce_sum | solution.py:18
  9.2 0.0 copy-done.2
  9.2 12.0 %all-gather = bf16[8,4,3584]{2,1,0:T(4,128)(2,1)} all-gather(bf16[1,4,3584]{2,1,0:T(4,128)(2,1)S(1)} %bitcast.12), channel_id=1, replica_groups=mesh['section'=4,'tensor'=8] {'tensor'}, dimensions={0}, use_global_device_ids=true | all-gather | bytes 258048 | tf_op jit(solution)/shard_map/all_gather | solution.py:10
  21.2 1.0 reshape.22
  22.2 0.0 copy-done
  22.2 0.0 copy-done.6
  22.2 1.2 fusion.5
  23.4 1.2 fusion.7
  24.5 0.0 all-reduce.4.cloned.1.call-update
  24.5 39.9 %psum.31 = f32[]{:T(128)} all-reduce(f32[]{:T(128)} %get-tuple-element.7), channel_id=1, replica_groups=mesh['section'=4,'tensor'=8] {'section','tensor'}, use_global_device_ids=true, to_apply=%region_9.0 | all-reduce | flops 1 | bytes 8 | tf_op jit(solution)/shard_map/psum | solution.py:19
  64.4 0.6 dynamic-slice
  65.7 14.0 %all-reduce.4.cloned.1.call-done = f32[32,3584]{1,0:T(8,128)} async-done(((f32[32,3584]{1,0:T(8,128)}), f32[32,3584]{1,0:T(8,128)}) %all-reduce.4.cloned.1.call-update) | async-done | bytes 458768
  79.7 0.9 constant_dynamic-slice_fusion
  80.6 19.6 %psum.28 = f32[4,3584]{1,0:T(4,128)S(1)} all-reduce(f32[4,3584]{1,0:T(4,128)S(1)} %constant_dynamic-slice_fusion), channel_id=1, replica_groups=mesh['section'=4,'tensor'=8] {'section'}, use_global_device_ids=true, to_apply=%region_1.0 | all-reduce | flops 14336 | bytes 114688 | tf_op jit(solution)/shard_map/psum | solution.py:28
  100.2 0.7 multiply_reduce_fusion
  101.0 9.6 %all-gather.1 = bf16[8,4,3584]{2,1,0:T(4,128)(2,1)} all-gather(bf16[1,4,3584]{2,1,0:T(4,128)(2,1)S(1)} %convert_bitcast_fusion), channel_id=1, replica_groups=mesh['section'=4,'tensor'=8] {'tensor'}, dimensions={0}, use_global_device_ids=true | all-gather | bytes 258048 | tf_op jit(solution)/shard_map/all_gather | solution.py:32
  110.6 1.0 reshape.24
  111.6 1.2 convolution_add_fusion.1
  112.8 1.8 %fusion = bf16[224,3584]{1,0:T(8,128)(2,1)} fusion(bf16[32,224]{1,0:T(8,128)(2,1)S(1)} %get-tuple-element.12, bf16[32,3584]{1,0:T(8,128)(2,1)S(1)} %reshape.24, bf16[224,3584]{1,0:T(8,128)(2,1)S(1)} %copy-done.1, f32[224]{0:T(256)S(1)} %add_sqrt_fusion, f32[224]{0:T(256)S(1)} %get-tuple-element.8), kind=kOutput, calls=%fused_computation.1 | convolution fusion | flops 55394304 | bytes 3456768 | tf_op jit(solution)/shard_map/dot_general | solution.py:35
  114.6 24.8 %all-reduce.1 = (f32[3584]{0:T(1024)}, f32[]{:T(128)}) all-reduce(f32[3584]{0:T(1024)S(1)} %copy-done.4, f32[]{:T(128)} %get-tuple-element.5), channel_id=1, replica_groups=mesh['section'=4,'tensor'=8] {'tensor'}, use_global_device_ids=true, to_apply=%region_5.0 | all-reduce | flops 3585 | bytes 28680 | tf_op jit(solution)/shard_map/psum | solution.py:31
  (12 shorter events, 0.0 us)
Async XLA Ops:
  7.2 15.0 %copy-start = (bf16[224,3584]{1,0:T(8,128)(2,1)S(1)}, bf16[224,3584]{1,0:T(8,128)(2,1)}, u32[]{:S(2)}) copy-start(bf16[224,3584]{1,0:T(8,128)(2,1)} %param.6) | copy-start | bytes 4816900
  7.2 2.0 %copy-start.2 = (bf16[4,3584]{1,0:T(4,128)(2,1)S(1)}, bf16[4,3584]{1,0:T(4,128)(2,1)}, u32[]{:S(2)}) copy-start(bf16[4,3584]{1,0:T(4,128)(2,1)} %param.5) | copy-start | bytes 86020
  7.2 15.0 %copy-start.6 = (f32[224]{0:T(256)S(1)}, f32[224]{0:T(256)}, u32[]{:S(2)}) copy-start(f32[224]{0:T(256)} %param.7) | copy-start | bytes 2692
  7.2 72.5 %all-reduce.4.cloned.1.call-start = ((), (), s32[]{:S(2)}) async-start(), calls=%async_computation | async-start | bytes 917504
  9.2 14.2 %copy-start.1 = (bf16[224,3584]{1,0:T(8,128)(2,1)S(1)}, bf16[224,3584]{1,0:T(8,128)(2,1)}, u32[]{:S(2)}) copy-start(bf16[224,3584]{1,0:T(8,128)(2,1)} %param.8) | copy-start | bytes 4816900
  23.4 41.1 %copy-start.7 = (u32[32]{0:T(128)S(1)}, u32[32]{0:T(128)}, u32[]{:S(2)}) copy-start(u32[32]{0:T(128)} %constant.13) | copy-start | bytes 388
  23.4 76.8 %copy-start.5 = (f32[3584]{0:T(1024)S(1)}, f32[3584]{0:T(1024)}, u32[]{:S(2)}) copy-start(f32[3584]{0:T(1024)} %param.9) | copy-start | bytes 43012
  100.9 13.6 %copy-start.3 = (f32[4,3584]{1,0:T(4,128)}, f32[4,3584]{1,0:T(4,128)S(1)}, u32[]{:S(2)}) copy-start(f32[4,3584]{1,0:T(4,128)S(1)} %get-tuple-element.11) | copy-start | bytes 172036
  112.8 1.8 %copy-start.4 = (f32[3584]{0:T(1024)S(1)}, f32[3584]{0:T(1024)}, u32[]{:S(2)}) copy-start(f32[3584]{0:T(1024)} %get-tuple-element.6) | copy-start | bytes 43012
Sparse Core Ops, SparseCore 0:
  24.7 54.9 all-reduce.3
where the time goes:
time: 149 us
  blocking collectives  106 us (71%)
  between operations  17.2 us (12%)
  waiting for transfers between devices  14 us (9%)
  matrix products  5.33 us (4%)
  local copies, waits for them, and re-layouts  3.52 us (2%)
  other arithmetic  2.7 us (2%)
    psum x1, blocking collectives, per_device(): penalty = lax.psum(jnp.sum(codes_f32 * dec_norm), ('section', 'tensor'))  39.9 us
    psum x1, blocking collectives, per_device(): lax.psum((jnp.sum(errors * errors), jnp.sum(errors, axis=0)), 'tensor')  24.8 us
    psum x1, blocking collectives, per_device(): shares = lax.psum(shares, 'section')  19.6 us
    unnamed x2, waiting for transfers between devices  14 us
    all_gather x1, blocking collectives, per_device(): stream = lax.all_gather(resid, 'tensor', axis=0, tiled=True)  12 us
    all_gather x1, blocking collectives, per_device(): lax.all_gather(errors.astype(jnp.bfloat16), 'tensor', axis=0, tiled=True)  9.61 us
    unnamed x20, local copies, waits for them, and re-layouts  3.52 us
  transfers between devices with their start and end apart: 1, of which 1 were waited for; matrix products, arithmetic and copies ran while one was open for 0% of the time, Pallas kernels for 0%

commit v1 on v0

--- a/solution.py
+++ b/solution.py
@@ -4,6 +4,15 @@
 from jax.sharding import PartitionSpec as P
 
 epsilon = 1e-06
+
+
+def added_up(value, mesh_axis):
+    size = lax.axis_size(mesh_axis)
+    total, hop = (value, 1)
+    while hop < size:
+        total = total + lax.ppermute(total, mesh_axis, [(i, i ^ hop) for i in range(size)])
+        hop = 2 * hop
+    return total
 
 
 def per_device(resid, w_enc, b_enc, w_dec, b_dec):
@@ -25,7 +34,7 @@
         scatter_dimension=0,
         tiled=True,
     )
-    shares = lax.psum(shares, "section")
+    shares = added_up(shares, "section")
     recon = shares + b_dec
     errors = recon - resid.astype(jnp.float32)
     squares, grad_b_dec = lax.psum((jnp.sum(errors * errors), jnp.sum(errors, axis=0)), "tensor")

time: 149 us -> 178 us (1.19)
  waiting for transfers between devices: 14 us -> 56.6 us
  blocking collectives: 106 us -> 87.4 us
  starting transfers between devices: 0.04 us -> 3.92 us
    unnamed x2, waiting for transfers between devices: 14 us -> 53.8 us
    psum x1 -> x0, blocking collectives: 19.6 us -> none  [per_device(): shares = lax.psum(shares, 'section')]
    ppermute x0 -> x2, starting transfers between devices: none -> 3.88 us  [added_up(): lax.ppermute(total, mesh_axis, [(i, i ^ hop) for i in range(size)])]
    ppermute x0 -> x2, waiting for transfers between devices: none -> 2.76 us  [added_up(): lax.ppermute(total, mesh_axis, [(i, i ^ hop) for i in range(size)])]
  transfers between devices with their start and end apart: 1 -> 3, of which waited for: 1 -> 2; matrix products, arithmetic and copies ran while one was open for 0% -> 0% of each run, Pallas kernels for 0% -> 0%
where the time goes in v1:
time: 178 us
  blocking collectives  87.4 us (49%)
  waiting for transfers between devices  56.6 us (32%)
  between operations  17.1 us (10%)
  matrix products  5.34 us (3%)
  starting transfers between devices  3.92 us (2%)
  other arithmetic  3.63 us (2%)
  local copies, waits for them, and re-layouts  3.52 us (2%)
    unnamed x2, waiting for transfers between devices  53.8 us
    psum x1, blocking collectives, per_device(): penalty = lax.psum(jnp.sum(codes_f32 * dec_norm), ('section', 'tensor'))  39.4 us
    psum x1, blocking collectives, per_device(): lax.psum((jnp.sum(errors * errors), jnp.sum(errors, axis=0)), 'tensor')  24.8 us
    all_gather x1, blocking collectives, per_device(): stream = lax.all_gather(resid, 'tensor', axis=0, tiled=True)  12 us
    all_gather x1, blocking collectives, per_device(): lax.all_gather(errors.astype(jnp.bfloat16), 'tensor', axis=0, tiled=True)  11.2 us
    ppermute x2, starting transfers between devices, added_up(): lax.ppermute(total, mesh_axis, [(i, i ^ hop) for i in range(size)])  3.88 us
  transfers between devices with their start and end apart: 3, of which 2 were waited for; matrix products, arithmetic and copies ran while one was open for 0% of the time, Pallas kernels for 0%

profile of v1, /device:TPU:0, one launch (start us, length us, event | category | flops | bytes accessed | tf_op | source)
XLA Modules:
  0.0 177.5 jit_solution(13409253331796959370)
XLA Ops:
  7.2 0.0 copy-start
  7.2 0.0 copy-start.2
  7.2 0.0 all-reduce.4.cloned.1.call-start
  7.2 1.9 %fusion.2 = f32[224]{0:T(256)S(1)} fusion(bf16[224,3584]{1,0:T(8,128)(2,1)} %param.8), kind=kLoop, calls=%fused_computation.5 | loop fusion | flops 2408224 | bytes 1606528 | tf_op jit(solution)/shard_map/reduce_sum | solution.py:27
  9.2 12.0 %all-gather = bf16[8,4,3584]{2,1,0:T(4,128)(2,1)} all-gather(bf16[1,4,3584]{2,1,0:T(4,128)(2,1)S(1)} %bitcast.12), channel_id=1, replica_groups=mesh['section'=4,'tensor'=8] {'tensor'}, dimensions={0}, use_global_device_ids=true | all-gather | bytes 258048 | tf_op jit(solution)/shard_map/all_gather | solution.py:19
  21.2 1.0 reshape.22
  22.2 1.2 fusion.5
  23.4 1.2 fusion.7
  24.5 0.0 all-reduce.4.cloned.1.call-update
  24.6 0.6 dynamic-slice
  25.8 53.8 %all-reduce.4.cloned.1.call-done = f32[32,3584]{1,0:T(8,128)} async-done(((f32[32,3584]{1,0:T(8,128)}), f32[32,3584]{1,0:T(8,128)}) %all-reduce.4.cloned.1.call-update) | async-done | bytes 458768
  79.6 0.9 constant_dynamic-slice_fusion
  80.5 1.5 collective-permute-start
  82.0 2.8 %collective-permute-done = f32[4,3584]{1,0:T(4,128)S(1)} collective-permute-done((f32[4,3584]{1,0:T(4,128)S(1)}, f32[4,3584]{1,0:T(4,128)S(1)}, u32[]{:S(2)}, u32[]{:S(2)}) %collective-permute-start) | collective-permute-done | bytes 57376 | tf_op jit(solution)/shard_map/ppermute | solution.py:13
  84.8 0.9 fusion.16
  85.7 2.4 %collective-permute-start.1 = (f32[4,3584]{1,0:T(4,128)S(1)}, f32[4,3584]{1,0:T(4,128)S(1)}, u32[]{:S(2)}, u32[]{:S(2)}) collective-permute-start(f32[4,3584]{1,0:T(4,128)S(1)} %fusion.16), channel_id=1, source_target_pairs={{0,16},{8,24},{16,0},{24,8},{1,17},{9,25},{17,1},{25,9},{2,18},{10... | collective-permute-start | bytes 172040 | tf_op jit(solution)/shard_map/ppermute | solution.py:13
  88.1 39.4 %psum.23 = f32[]{:T(128)} all-reduce(f32[]{:T(128)} %get-tuple-element.7), channel_id=1, replica_groups=mesh['section'=4,'tensor'=8] {'section','tensor'}, use_global_device_ids=true, to_apply=%region_8.0 | all-reduce | flops 1 | bytes 8 | tf_op jit(solution)/shard_map/psum | solution.py:28
  127.5 0.0 collective-permute-done.1
  127.5 0.8 multiply_reduce_fusion
  128.3 11.2 %all-gather.1 = bf16[8,4,3584]{2,1,0:T(4,128)(2,1)} all-gather(bf16[1,4,3584]{2,1,0:T(4,128)(2,1)S(1)} %convert_bitcast_fusion), channel_id=1, replica_groups=mesh['section'=4,'tensor'=8] {'tensor'}, dimensions={0}, use_global_device_ids=true | all-gather | bytes 258048 | tf_op jit(solution)/shard_map/all_gather | solution.py:41
  139.5 1.0 reshape.24
  140.5 1.2 convolution_add_fusion.1
  141.7 1.8 %fusion = bf16[224,3584]{1,0:T(8,128)(2,1)} fusion(bf16[32,224]{1,0:T(8,128)(2,1)S(1)} %get-tuple-element.12, bf16[32,3584]{1,0:T(8,128)(2,1)S(1)} %reshape.24, bf16[224,3584]{1,0:T(8,128)(2,1)S(1)} %copy-done.1, f32[224]{0:T(256)S(1)} %add_sqrt_fusion, f32[224]{0:T(256)S(1)} %get-tuple-element.8), kind=kOutput, calls=%fused_computation.1 | convolution fusion | flops 55394304 | bytes 3456768 | tf_op jit(solution)/shard_map/dot_general | solution.py:44
  143.5 24.8 %all-reduce.1 = (f32[3584]{0:T(1024)}, f32[]{:T(128)}) all-reduce(f32[3584]{0:T(1024)S(1)} %copy-done.4, f32[]{:T(128)} %get-tuple-element.5), channel_id=1, replica_groups=mesh['section'=4,'tensor'=8] {'tensor'}, use_global_device_ids=true, to_apply=%region_4.0 | all-reduce | flops 3585 | bytes 28680 | tf_op jit(solution)/shard_map/psum | solution.py:40
  (16 shorter events, 0.1 us)
Async XLA Ops:
  7.2 15.0 %copy-start = (bf16[224,3584]{1,0:T(8,128)(2,1)S(1)}, bf16[224,3584]{1,0:T(8,128)(2,1)}, u32[]{:S(2)}) copy-start(bf16[224,3584]{1,0:T(8,128)(2,1)} %param.6) | copy-start | bytes 4816900
  7.2 2.0 %copy-start.2 = (bf16[4,3584]{1,0:T(4,128)(2,1)S(1)}, bf16[4,3584]{1,0:T(4,128)(2,1)}, u32[]{:S(2)}) copy-start(bf16[4,3584]{1,0:T(4,128)(2,1)} %param.5) | copy-start | bytes 86020
  7.2 15.0 %copy-start.6 = (f32[224]{0:T(256)S(1)}, f32[224]{0:T(256)}, u32[]{:S(2)}) copy-start(f32[224]{0:T(256)} %param.7) | copy-start | bytes 2692
  7.2 72.4 %all-reduce.4.cloned.1.call-start = ((), (), s32[]{:S(2)}) async-start(), calls=%async_computation | async-start | bytes 917504
  9.2 14.2 %copy-start.1 = (bf16[224,3584]{1,0:T(8,128)(2,1)S(1)}, bf16[224,3584]{1,0:T(8,128)(2,1)}, u32[]{:S(2)}) copy-start(bf16[224,3584]{1,0:T(8,128)(2,1)} %param.8) | copy-start | bytes 4816900
  23.4 1.2 copy-start.7
  23.4 104.1 %copy-start.5 = (f32[3584]{0:T(1024)S(1)}, f32[3584]{0:T(1024)}, u32[]{:S(2)}) copy-start(f32[3584]{0:T(1024)} %param.9) | copy-start | bytes 43012
  80.5 4.2 %collective-permute-start = (f32[4,3584]{1,0:T(4,128)S(1)}, f32[4,3584]{1,0:T(4,128)S(1)}, u32[]{:S(2)}, u32[]{:S(2)}) collective-permute-start(f32[4,3584]{1,0:T(4,128)S(1)} %constant_dynamic-slice_fusion), channel_id=1, source_target_pairs={{0,8},{8,0},{16,24},{24,16},{1,9},{9,1},{17,25},{25,17},{2,10},{10... | collective-permute-start | bytes 172040 | tf_op jit(solution)/shard_map/ppermute | solution.py:13
  85.7 41.8 %collective-permute-start.1 = (f32[4,3584]{1,0:T(4,128)S(1)}, f32[4,3584]{1,0:T(4,128)S(1)}, u32[]{:S(2)}, u32[]{:S(2)}) collective-permute-start(f32[4,3584]{1,0:T(4,128)S(1)} %fusion.16), channel_id=1, source_target_pairs={{0,16},{8,24},{16,0},{24,8},{1,17},{9,25},{17,1},{25,9},{2,18},{10... | collective-permute-start | bytes 172040 | tf_op jit(solution)/shard_map/ppermute | solution.py:13
  128.3 15.3 %copy-start.3 = (f32[4,3584]{1,0:T(4,128)}, f32[4,3584]{1,0:T(4,128)S(1)}, u32[]{:S(2)}) copy-start(f32[4,3584]{1,0:T(4,128)S(1)} %get-tuple-element.11) | copy-start | bytes 172036
  141.7 1.8 %copy-start.4 = (f32[3584]{0:T(1024)S(1)}, f32[3584]{0:T(1024)}, u32[]{:S(2)}) copy-start(f32[3584]{0:T(1024)} %get-tuple-element.6) | copy-start | bytes 43012
Sparse Core Ops, SparseCore 0:
  24.7 54.9 all-reduce.3
